TPU v7x, 32 devices: a whole 2x2x4 slice. The times are simulated.
32 devices in a mesh: dp: 16 (over z, x, core), tp: 2 (over y).
Axes of the slice: x: 2, y: 2, z: 4, core: 2. Of those that a mesh axis runs over, the one named last changes fastest.
Arguments:
- inputs: bfloat16 [32768, 640], P('dp'), may hold values from -6 to 6
- out_grad: bfloat16 [32768, 640], P('dp'), may hold values from -6 to 6
- segment_ids: int32 [32, 1024], P('dp'), may hold values from 0 to 5, never falling along the last dimension, each value on 1 to 400 neighbouring positions
- attn_weights: float32 [4, 640, 640], P(None, 'dp', 'tp'), may hold values from -6 to 6
- ffn_weights: float32 [2, 640, 2560], P(None, 'dp', 'tp'), may hold values from -4 to 4
- head_bias: float32 [3, 640], P(None, 'tp'), may hold values from -1 to 1
- hidden_bias: float32 [2560], P('tp'), may hold values from -1 to 1
- norm_vectors: float32 [6, 640], replicated, may hold values from -1 to 2
- attn_first: float32 [4, 640, 640], P(None, 'dp', 'tp')
- ffn_first: float32 [2, 640, 2560], P(None, 'dp', 'tp')
- head_first: float32 [3, 640], P(None, 'tp')
- hidden_first: float32 [2560], P('tp')
- vector_first: float32 [6, 640], replicated
- attn_second: float32 [4, 640, 640], P(None, 'dp', 'tp')
- ffn_second: float32 [2, 640, 2560], P(None, 'dp', 'tp')
- head_second: float32 [3, 640], P(None, 'tp')
- hidden_second: float32 [2560], P('tp')
- vector_second: float32 [6, 640], replicated
Outputs:
- layer_output: bfloat16 [32768, 640], P('dp')
- input_grad: bfloat16 [32768, 640], P('dp')
- new_attn_weights: float32 [4, 640, 640], P(None, 'dp', 'tp')
- new_ffn_weights: float32 [2, 640, 2560], P(None, 'dp', 'tp')
- new_head_bias: float32 [3, 640], P(None, 'tp')
- new_hidden_bias: float32 [2560], P('tp')
- new_norm_vectors: float32 [6, 640], replicated
- attn_first_new: float32 [4, 640, 640], P(None, 'dp', 'tp')
- ffn_first_new: float32 [2, 640, 2560], P(None, 'dp', 'tp')
- head_first_new: float32 [3, 640], P(None, 'tp')
- hidden_first_new: float32 [2560], P('tp')
- vector_first_new: float32 [6, 640], replicated
- attn_second_new: float32 [3, 640, 640], P(None, 'dp', 'tp')
- out_second_new: float32 [640, 640], P('dp', 'tp')
- ffn_second_new: float32 [2, 640, 2560], P(None, 'dp', 'tp')
- head_second_new: float32 [3, 640], P(None, 'tp')
- hidden_second_new: float32 [2560], P('tp')
- vector_second_new: float32 [4, 640], replicated
- norm_second_new: float32 [2, 640], replicated
- trust_norms: float32 [2, 16], replicated
Inputs may be any that keep to these rules, and one draw needn't show every extreme that they name: `segment_ids`: within each row of 1024 slots the ids never fall; each of the 6 ids forms one run of 1 to 400 slots, and one run has exactly 400 slots.
All inputs are finite; a program needn't handle non-finite values.
Results may differ from a plain program's by a relative error of at most 0.019.
Values may be sent and summed in bfloat16 or wider, within the bound.
No kernel may reach another device: no remote copies, remote signals or barrier semaphores. Data moves between devices by JAX's collectives and lax.ppermute only.
A program may use at most 192 MiB of HBM per device.

v0:
```python
from functools import partial
import jax
import jax.numpy as jnp
from jax import lax
from jax.sharding import PartitionSpec as P

HD = 32
STEP = 10
EPS_NORM = 1e-05
EPS_ADAM = 1e-06
BETA_ONE = 0.9
BETA_TWO = 0.999
DECAY = 0.01
RATE = 0.5
MASKED = -1e30


def layer_norm(values, scale_gain, offset):
    average = jnp.mean(values, axis=-1, keepdims=True)
    centered = values - average
    variance = jnp.mean(centered * centered, axis=-1, keepdims=True)
    return centered * lax.rsqrt(variance + EPS_NORM) * scale_gain + offset


def rope_tables(segments):
    slots_index = jnp.arange(segments.shape[0], dtype=jnp.int32)
    before = jnp.sum((segments[None, :] < segments[:, None]).astype(jnp.int32), axis=1)
    position = (slots_index - before).astype(jnp.float32)
    frequency = 10000.0 ** (-jnp.arange(0, HD, 2).astype(jnp.float32) / HD)
    angles = position[:, None] * frequency[None, :]
    angles = jnp.concatenate([angles, angles], axis=-1)
    return (jnp.cos(angles), jnp.sin(angles))


def rotate(values, cosine_table, sine_table):
    middle = values.shape[-1] // 2
    turned = jnp.concatenate([-values[..., middle:], values[..., :middle]], axis=-1)
    return values * cosine_table + turned * sine_table


def block_scores(queries, keys_row, same_protein):
    scores = jnp.einsum(
        "qhd,khd->hqk", queries, keys_row, preferred_element_type=jnp.float32
    ) * HD ** (-0.5)
    return jnp.where(same_protein[None], scores, MASKED)


def attend_block(queries, keys_row, values_row, same_protein):
    scores = block_scores(queries, keys_row, same_protein)
    highest = jnp.max(scores, axis=-1, keepdims=True)
    weights_exp = jnp.exp(scores - highest)
    row_total = jnp.sum(weights_exp, axis=-1, keepdims=True)
    attention = (weights_exp / row_total).astype(jnp.bfloat16)
    heads_out = jnp.einsum(
        "hqk,khd->qhd", attention, values_row, preferred_element_type=jnp.float32
    )
    return (heads_out, (highest + jnp.log(row_total))[..., 0])


def attend_block_back(queries, keys_row, values_row, same_protein, log_total, grad_heads):
    scores = block_scores(queries, keys_row, same_protein)
    attention = jnp.exp(scores - log_total[..., None])
    grad_values = jnp.einsum(
        "hqk,qhd->khd",
        attention.astype(jnp.bfloat16),
        grad_heads,
        preferred_element_type=jnp.float32,
    )
    grad_attention = jnp.einsum(
        "qhd,khd->hqk", grad_heads, values_row, preferred_element_type=jnp.float32
    )
    center = jnp.sum(attention * grad_attention, axis=-1, keepdims=True)
    grad_scores = (attention * (grad_attention - center)).astype(jnp.bfloat16)
    grad_queries = jnp.einsum(
        "hqk,khd->qhd", grad_scores, keys_row, preferred_element_type=jnp.float32
    ) * HD ** (-0.5)
    grad_keys = jnp.einsum(
        "hqk,qhd->khd", grad_scores, queries, preferred_element_type=jnp.float32
    ) * HD ** (-0.5)
    return (grad_queries, grad_keys, grad_values)


def attend_row(queries, keys_row, values_row, segments, block_rows):
    blocks = segments.shape[0] // block_rows
    query_blocks = queries.reshape((blocks, block_rows) + queries.shape[1:])
    segment_blocks = segments.reshape(blocks, block_rows)

    def one_block(packed):
        same_protein = packed[1][:, None] == segments[None, :]
        return attend_block(packed[0], keys_row, values_row, same_protein)

    heads_out, log_total = lax.map(one_block, (query_blocks, segment_blocks))
    return (heads_out.reshape(queries.shape), log_total)


def attend_row_back(queries, keys_row, values_row, segments, log_total, grad_heads, block_rows):
    blocks = segments.shape[0] // block_rows
    query_blocks = queries.reshape((blocks, block_rows) + queries.shape[1:])
    grad_blocks = grad_heads.reshape((blocks, block_rows) + grad_heads.shape[1:])
    segment_blocks = segments.reshape(blocks, block_rows)

    def one_block(totals, packed):
        same_protein = packed[1][:, None] == segments[None, :]
        grad_queries, grad_keys, grad_values = attend_block_back(
            packed[0], keys_row, values_row, same_protein, packed[2], packed[3]
        )
        return ((totals[0] + grad_keys, totals[1] + grad_values), grad_queries)

    zeros_rows = jnp.zeros(keys_row.shape, jnp.float32)
    sums_kv, grad_queries = lax.scan(
        one_block, (zeros_rows, zeros_rows), (query_blocks, segment_blocks, log_total, grad_blocks)
    )
    return (grad_queries.reshape(queries.shape), sums_kv[0], sums_kv[1])


def lamb_moments(weight, gradient, moment_one, moment_two):
    first_new = BETA_ONE * moment_one + (1.0 - BETA_ONE) * gradient
    second_new = BETA_TWO * moment_two + (1.0 - BETA_TWO) * gradient * gradient
    corrected = first_new / (1.0 - BETA_ONE**STEP)
    variance = second_new / (1.0 - BETA_TWO**STEP)
    update = corrected / (jnp.sqrt(variance) + EPS_ADAM) + DECAY * weight
    return (first_new, second_new, update)


def sum_squares(array):
    return jnp.sum(array * array, axis=tuple(range(1, array.ndim)))


def on_device(
    inputs,
    out_grad,
    segment_ids,
    attn_weights,
    ffn_weights,
    head_bias,
    hidden_bias,
    norm_vectors,
    attn_first,
    ffn_first,
    head_first,
    hidden_first,
    vector_first,
    attn_second,
    ffn_second,
    head_second,
    hidden_second,
    vector_second,
):
    data_count = lax.axis_size("dp")
    tensor_count = lax.axis_size("tp")
    row_count, slot_count = segment_ids.shape
    token_count = row_count * slot_count
    head_width = attn_weights.shape[2]
    local_heads = head_width // HD
    block_rows = min(512, slot_count)
    shard_rows = attn_weights.shape[1]
    masters = [attn_weights, ffn_weights, head_bias, hidden_bias.reshape(1, -1), norm_vectors]
    replicas = [1.0, 1.0, 1.0 / data_count, 1.0 / data_count, 1.0 / (data_count * tensor_count)]
    weight_terms = jnp.concatenate(
        [sum_squares(masters[member]) * replicas[member] for member in range(5)]
    )
    weight_sums = lax.psum(weight_terms, ("dp", "tp"))
    gathered_attn, gathered_ffn = (
        lax.all_gather(attn_weights.astype(jnp.bfloat16), "dp", axis=1, tiled=True),
        lax.all_gather(ffn_weights.astype(jnp.bfloat16), "dp", axis=1, tiled=True),
    )
    tables = jax.vmap(rope_tables)(segment_ids)
    cosine_table = tables[0][:, :, None, :]
    sine_table = tables[1][:, :, None, :]
    features = inputs.astype(jnp.float32)
    normed, norm_back = jax.vjp(layer_norm, features, norm_vectors[0], norm_vectors[1])
    normed_low = normed.astype(jnp.bfloat16)
    projected = jnp.einsum(
        "td,cdw->ctw", normed_low, gathered_attn[:3], preferred_element_type=jnp.float32
    )
    projected = projected + head_bias[:, None, :]
    shaped = projected.reshape(3, row_count, slot_count, local_heads, HD)
    turned, rotate_back = jax.vjp(lambda pair: rotate(pair, cosine_table, sine_table), shaped[:2])
    turned_low = turned.astype(jnp.bfloat16)
    values_low = shaped[2].astype(jnp.bfloat16)
    heads_out, log_total = lax.map(
        lambda packed: attend_row(packed[0], packed[1], packed[2], packed[3], block_rows),
        (turned_low[0], turned_low[1], values_low, segment_ids),
    )
    heads_low = heads_out.reshape(token_count, head_width).astype(jnp.bfloat16)
    out_projection = gathered_attn[3]
    attended = lax.psum(
        jnp.einsum(
            "tw,dw->td", heads_low, out_projection, preferred_element_type=jnp.float32
        ).astype(jnp.bfloat16),
        "tp",
    ).astype(jnp.float32)
    residual = features + attended + norm_vectors[2]
    normed_two, norm_two_back = jax.vjp(layer_norm, residual, norm_vectors[3], norm_vectors[4])
    normed_two_low = normed_two.astype(jnp.bfloat16)
    preact = (
        jnp.dot(normed_two_low, gathered_ffn[0], preferred_element_type=jnp.float32) + hidden_bias
    )
    activated, gelu_back = jax.vjp(partial(jax.nn.gelu, approximate=False), preact)
    activated_low = activated.astype(jnp.bfloat16)
    mixed_sum = lax.psum(
        jnp.einsum(
            "tf,df->td", activated_low, gathered_ffn[1], preferred_element_type=jnp.float32
        ).astype(jnp.bfloat16),
        "tp",
    ).astype(jnp.float32)
    layer_output = (residual + mixed_sum + norm_vectors[5]).astype(jnp.bfloat16)
    grad_output = out_grad.astype(jnp.float32)
    grad_down = jnp.einsum("td,tf->df", out_grad, activated_low, preferred_element_type=jnp.float32)
    grad_act = jnp.einsum(
        "td,df->tf", out_grad, gathered_ffn[1], preferred_element_type=jnp.float32
    )
    grad_pre = gelu_back(grad_act)[0].astype(jnp.bfloat16)
    grad_up = jnp.einsum("td,tf->df", normed_two_low, grad_pre, preferred_element_type=jnp.float32)
    grad_hidden_bias = jnp.sum(grad_pre.astype(jnp.float32), axis=0)
    grad_normed_two = lax.psum(
        jnp.einsum(
            "tf,df->td", grad_pre, gathered_ffn[0], preferred_element_type=jnp.float32
        ).astype(jnp.bfloat16),
        "tp",
    ).astype(jnp.float32)
    grad_residual_ln, grad_gain_two, grad_shift_two = norm_two_back(grad_normed_two)
    grad_residual = grad_output + grad_residual_ln
    grad_residual_low = grad_residual.astype(jnp.bfloat16)
    grad_out_projection = jnp.einsum(
        "td,tw->dw", grad_residual_low, heads_low, preferred_element_type=jnp.float32
    )
    grad_heads = jnp.einsum(
        "td,dw->tw", grad_residual_low, out_projection, preferred_element_type=jnp.float32
    )
    grad_heads = grad_heads.astype(jnp.bfloat16).reshape(row_count, slot_count, local_heads, HD)
    grad_turned_q, grad_turned_k, grad_values = lax.map(
        lambda packed: attend_row_back(
            packed[0], packed[1], packed[2], packed[3], packed[4], packed[5], block_rows
        ),
        (turned_low[0], turned_low[1], values_low, segment_ids, log_total, grad_heads),
    )
    grad_shaped_qk = rotate_back(jnp.stack([grad_turned_q, grad_turned_k]))[0]
    grad_projected = jnp.concatenate([grad_shaped_qk, grad_values[None]], axis=0)
    grad_projected = grad_projected.reshape(3, token_count, head_width).astype(jnp.bfloat16)
    grad_head_bias = jnp.sum(grad_projected.astype(jnp.float32), axis=1)
    grad_qkv = jnp.einsum(
        "td,ctw->cdw", normed_low, grad_projected, preferred_element_type=jnp.float32
    )
    grad_normed = lax.psum(
        jnp.einsum(
            "ctw,cdw->td", grad_projected, gathered_attn[:3], preferred_element_type=jnp.float32
        ).astype(jnp.bfloat16),
        "tp",
    ).astype(jnp.float32)
    grad_features_ln, grad_gain, grad_shift = norm_back(grad_normed)
    input_grad = (grad_residual + grad_features_ln).astype(jnp.bfloat16)
    grad_vectors = jnp.stack(
        [
            grad_gain,
            grad_shift,
            jnp.sum(grad_residual, axis=0),
            grad_gain_two,
            grad_shift_two,
            jnp.sum(grad_output, axis=0),
        ]
    )
    grad_attn = jnp.concatenate([grad_qkv, grad_out_projection[None]], axis=0)
    grad_ffn = jnp.stack([grad_up, grad_down])
    full_attn, full_ffn, sum_head, sum_hidden, sum_vectors = lax.psum(
        (grad_attn, grad_ffn, grad_head_bias, grad_hidden_bias, grad_vectors), "dp"
    )
    offset_rows = lax.axis_index("dp") * shard_rows
    own_attn = lax.dynamic_slice_in_dim(full_attn, offset_rows, shard_rows, 1)
    own_ffn = lax.dynamic_slice_in_dim(full_ffn, offset_rows, shard_rows, 1)
    grads_list = [own_attn, own_ffn, sum_head, sum_hidden.reshape(1, -1), sum_vectors]
    firsts = [attn_first, ffn_first, head_first, hidden_first.reshape(1, -1), vector_first]
    seconds = [attn_second, ffn_second, head_second, hidden_second.reshape(1, -1), vector_second]
    results = [
        lamb_moments(masters[member], grads_list[member], firsts[member], seconds[member])
        for member in range(5)
    ]
    update_terms = jnp.concatenate(
        [sum_squares(results[member][2]) * replicas[member] for member in range(5)]
    )
    update_sums = lax.psum(update_terms, ("dp", "tp"))
    weight_norms = jnp.sqrt(weight_sums)
    update_norms = jnp.sqrt(update_sums)
    trust_ratio = weight_norms / update_norms
    counts = [4, 2, 3, 1, 6]
    new_weights = []
    begin_at = 0
    for member in range(5):
        piece_ratio = trust_ratio[begin_at : begin_at + counts[member]]
        shaped_ratio = piece_ratio.reshape((-1,) + (1,) * (masters[member].ndim - 1))
        new_weights.append(masters[member] - RATE * shaped_ratio * results[member][2])
        begin_at += counts[member]
    return (
        layer_output,
        input_grad,
        new_weights[0],
        new_weights[1],
        new_weights[2],
        new_weights[3].reshape(-1),
        new_weights[4],
        results[0][0],
        results[1][0],
        results[2][0],
        results[3][0].reshape(-1),
        results[4][0],
        results[0][1][:3],
        results[0][1][3],
        results[1][1],
        results[2][1],
        results[3][1].reshape(-1),
        results[4][1][2:],
        results[4][1][:2],
        jnp.stack([weight_norms, update_norms]),
    )


def solution(mesh):
    in_specs = (
        P("dp", None),
        P("dp", None),
        P("dp", None),
        P(None, "dp", "tp"),
        P(None, "dp", "tp"),
        P(None, "tp"),
        P("tp"),
        P(),
        P(None, "dp", "tp"),
        P(None, "dp", "tp"),
        P(None, "tp"),
        P("tp"),
        P(),
        P(None, "dp", "tp"),
        P(None, "dp", "tp"),
        P(None, "tp"),
        P("tp"),
        P(),
    )
    out_specs = (
        P("dp", None),
        P("dp", None),
        P(None, "dp", "tp"),
        P(None, "dp", "tp"),
        P(None, "tp"),
        P("tp"),
        P(),
        P(None, "dp", "tp"),
        P(None, "dp", "tp"),
        P(None, "tp"),
        P("tp"),
        P(),
        P(None, "dp", "tp"),
        P("dp", "tp"),
        P(None, "dp", "tp"),
        P(None, "tp"),
        P("tp"),
        P(),
        P(),
        P(),
    )
    return jax.shard_map(
        on_device, mesh=mesh, in_specs=in_specs, out_specs=out_specs, check_vma=False
    )
```

profile of v0, /device:TPU:12, one launch (start us, length us, event | category | flops | bytes accessed | tf_op | source)
XLA Modules:
  0.0 1304.4 jit_solution(11081138493760027001)
XLA Ops:
  17.8 34.1 %all-gather.3.cloned.1.call-done = bf16[4,640,320]{2,0,1:T(4,128)(2,1)} async-done(((bf16[4,40,320]{2,0,1:T(4,128)(2,1)}), bf16[4,640,320]{2,0,1:T(4,128)(2,1)}) %all-gather.3.cloned.1.call-update) | async-done | bytes 1638416 | tf_op jit(solution)/shard_map/all_gather | solution.py:164
  51.9 4.5 copy.205
  56.4 4.8 add_bitcast_fusion
  67.5 8.1 slice.89
  88.0 138.8 %while.54 = (s32[]{:T(128)}, bf16[2,1024,10,32]{3,2,1,0:T(8,128)(2,1)}, f32[2,2,10,512]{3,2,1,0:T(8,128)}, bf16[2,1024,10,32]{1,3,2,0:T(8,128)(2,1)S(1)}, s32[2,...) while((s32[]{:T(128)}, ...), condition=%wide.region_8.0_spmd, body=%wide.region_3.8_spmd.sunk | while | flops 734522368 | bytes 181594624 | solution.py:181
  92.8 54.8 %while.57 = (s32[]{:T(128)}, bf16[2,512,10,32]{1,3,2,0:T(8,128)(2,1)S(1)}, f32[2,10,512]{2,1,0:T(8,128)S(1)}, s32[2,512]{1,0:T(2,128)S(1)}, s32[1024]{0:T(1024)S...) while((s32[]{:T(128)}, ...), condition=%wide.region_7.7_spmd, body=%wide.region_4.6_spmd.sunk | while | flops 734522368 | bytes 154048688 | solution.py:92
  97.3 7.0 copy-done.1
  104.2 6.2 fusion.156
  110.5 9.7 fusion.157
  124.7 7.0 copy-done.1
  131.6 6.2 fusion.156
  137.9 9.7 fusion.157
  147.7 4.7 copy.245
  152.4 5.0 bitcast_dynamic-update-slice_fusion.9
  162.2 54.8 %while.57 = (s32[]{:T(128)}, bf16[2,512,10,32]{1,3,2,0:T(8,128)(2,1)S(1)}, f32[2,10,512]{2,1,0:T(8,128)S(1)}, s32[2,512]{1,0:T(2,128)S(1)}, s32[1024]{0:T(1024)S...) while((s32[]{:T(128)}, ...), condition=%wide.region_7.7_spmd, body=%wide.region_4.6_spmd.sunk | while | flops 734522368 | bytes 154048688 | solution.py:92
  166.6 7.0 copy-done.1
  173.6 6.2 fusion.156
  179.8 9.7 fusion.157
  194.0 7.0 copy-done.1
  201.0 6.2 fusion.156
  207.2 9.7 fusion.157
  217.0 4.7 copy.245
  221.8 5.0 bitcast_dynamic-update-slice_fusion.9
  227.8 10.1 reshape.337
  237.9 4.7 convolution_convert_fusion.2
  243.5 72.7 %all-reduce.11.cloned.1.call-done = bf16[2048,640]{1,0:T(8,128)(2,1)} async-done(((bf16[2048,640]{1,0:T(8,128)(2,1)}), bf16[2048,640]{1,0:T(8,128)(2,1)}) %all-reduce.11.cloned.1.call-update) | async-done | bytes 2621456 | tf_op jit(solution)/shard_map/psum | solution.py:187
  320.5 46.1 %all-gather.5.cloned.1.call-done = bf16[2,640,1280]{2,1,0:T(8,128)(2,1)} async-done(((bf16[2,40,1280]{2,1,0:T(8,128)(2,1)}), bf16[2,640,1280]{2,1,0:T(8,128)(2,1)}) %all-gather.5.cloned.1.call-update) | async-done | bytes 3276816 | tf_op jit(solution)/shard_map/all_gather | solution.py:165
  366.6 31.1 %multiply_convert_fusion.1 = (bf16[2048,1280]{1,0:T(8,128)(2,1)}, f32[2048,1280]{1,0:T(8,128)}, f32[2048,1280]{1,0:T(8,128)}) fusion(f32[1280]{0:T(1024)S(1)} %copy-done.50, bf16[2,640,1280]{2,1,0:T(8,128)(2,1)} %all-gather.5.cloned.1.call-done, f32[640]{0:T(1024)S(1)} %copy-done.58, f32[640]{0:T(1024)S(1)} %copy-done.47, f32[2048]{0:T(1024)S(1)} %fusion.84, ...), kind=kOutput, calls=%fused_computation.69 | convolution fusion | flops 3540254720 | bytes 33124864 | tf_op jit(solution)/shard_map/dot_general | solution.py:197
  397.8 12.4 convert_reduce_fusion
  412.5 5.9 convolution_convert_fusion
  418.6 7.3 convolution_bitcast_fusion
  433.5 56.9 %all-reduce.13.cloned.1.call-done = bf16[2048,640]{1,0:T(8,128)(2,1)} async-done(((bf16[2048,640]{1,0:T(8,128)(2,1)}), bf16[2048,640]{1,0:T(8,128)(2,1)}) %all-reduce.13.cloned.1.call-update) | async-done | bytes 2621456 | tf_op jit(solution)/shard_map/psum | solution.py:216
  490.5 5.1 convert_reduce_fusion.4
  495.5 4.7 fusion.61
  510.4 277.2 %while.56 = (s32[]{:T(128)}, f32[2,1024,10,32]{1,3,2,0:T(8,128)}, f32[2,1024,10,32]{1,3,2,0:T(8,128)}, bf16[2,1024,10,32]{1,3,2,0:T(8,128)(2,1)}, bf16[2,1024,10...) while((s32[]{:T(128)}, f32[2,1024,10,32]{1,3,2,0:T(8,128)}, ...), condition=%wide.region_20.21_spmd, body=%wide.region_16.20_spmd.sunk | while | flops 1758686208 | bytes 284158464 | solution.py:232
  522.2 111.2 %while.58 = (s32[]{:T(128)}, f32[1024,10,32]{0,2,1:T(8,128)S(1)}, f32[1024,10,32]{0,2,1:T(8,128)}, f32[2,512,10,32]{1,3,2,0:T(8,128)}, bf16[2,512,10,32]{1,3,2,0...) while((s32[]{:T(128)}, f32[1024,10,32]{0,2,1:T(8,128)S(1)}, ...), condition=%wide.region_19.19_spmd.clone, body=%wide.region_17.18_spmd.clone.sunk | while | flops 1758686208 | bytes 255219920 | solution.py:110
  527.2 7.0 copy-done
  534.2 7.7 fusion.151
  541.9 15.2 %multiply_reduce_fusion.13 = (f32[10,512]{1,0:T(8,128)S(1)}, f32[10,512,1024]{2,1,0:T(8,128)}) fusion(f32[10,512,1024]{2,1,0:T(8,128)} %copy-done, f32[10,512]{1,0:T(8,128)S(1)} %dynamic-slice_bitcast_fusion.15, pred[512,1024]{1,0:T(8,128)(4,1)S(1)} %broadcast_compare_fusion.4, bf16[1024,10,32]{0,2,1:T(8,128)(2,1)} %get-tuple-element.1035, ...), kind=kOutput, calls=%fused_computation.18.clone.1 | convolution fusion | flops 361753600 | bytes 43491332 | tf_op jit(solution)/shard_map/while/body/eval_jaxpr/while/body/eval_jaxpr/qhd,khd->hqk/dot_general | solution.py:69
  557.0 14.6 %multiply_convert_fusion.3 = bf16[10,512,1024]{2,1,0:T(8,128)(2,1)S(1)} fusion(f32[10,512,1024]{2,1,0:T(8,128)} %get-tuple-element.987, f32[10,512,1024]{2,1,0:T(8,128)} %copy-done, f32[10,512]{1,0:T(8,128)S(1)} %get-tuple-element.988, f32[10,512]{1,0:T(8,128)S(1)} %dynamic-slice_bitcast_fusion.15, pred[512,1024]{1,0:T(8,128)(4,1)S(1)} %broadcast_compare_fusion.4), kind=kLoop, calls=%fused_computation.17.clone.1 | loop fusion | flops 31457280 | bytes 52994048 | tf_op jit(solution)/shard_map/while/body/eval_jaxpr/while/body/eval_jaxpr/convert_element_type | solution.py:73
  582.7 7.0 copy-done
  589.7 7.9 fusion.151
  597.6 15.2 %multiply_reduce_fusion.13 = (f32[10,512]{1,0:T(8,128)S(1)}, f32[10,512,1024]{2,1,0:T(8,128)}) fusion(f32[10,512,1024]{2,1,0:T(8,128)} %copy-done, f32[10,512]{1,0:T(8,128)S(1)} %dynamic-slice_bitcast_fusion.15, pred[512,1024]{1,0:T(8,128)(4,1)S(1)} %broadcast_compare_fusion.4, bf16[1024,10,32]{0,2,1:T(8,128)(2,1)} %get-tuple-element.1035, ...), kind=kOutput, calls=%fused_computation.18.clone.1 | convolution fusion | flops 361753600 | bytes 43491332 | tf_op jit(solution)/shard_map/while/body/eval_jaxpr/while/body/eval_jaxpr/qhd,khd->hqk/dot_general | solution.py:69
  612.8 14.6 %multiply_convert_fusion.3 = bf16[10,512,1024]{2,1,0:T(8,128)(2,1)S(1)} fusion(f32[10,512,1024]{2,1,0:T(8,128)} %get-tuple-element.987, f32[10,512,1024]{2,1,0:T(8,128)} %copy-done, f32[10,512]{1,0:T(8,128)S(1)} %get-tuple-element.988, f32[10,512]{1,0:T(8,128)S(1)} %dynamic-slice_bitcast_fusion.15, pred[512,1024]{1,0:T(8,128)(4,1)S(1)} %broadcast_compare_fusion.4), kind=kLoop, calls=%fused_computation.17.clone.1 | loop fusion | flops 31457280 | bytes 52994048 | tf_op jit(solution)/shard_map/while/body/eval_jaxpr/while/body/eval_jaxpr/convert_element_type | solution.py:73
  636.4 6.2 copy.248
  642.5 5.2 copy.249
  660.5 111.2 %while.58 = (s32[]{:T(128)}, f32[1024,10,32]{0,2,1:T(8,128)S(1)}, f32[1024,10,32]{0,2,1:T(8,128)}, f32[2,512,10,32]{1,3,2,0:T(8,128)}, bf16[2,512,10,32]{1,3,2,0...) while((s32[]{:T(128)}, f32[1024,10,32]{0,2,1:T(8,128)S(1)}, ...), condition=%wide.region_19.19_spmd.clone, body=%wide.region_17.18_spmd.clone.sunk | while | flops 1758686208 | bytes 255219920 | solution.py:110
  665.5 7.0 copy-done
  672.5 7.7 fusion.151
  680.2 15.2 %multiply_reduce_fusion.13 = (f32[10,512]{1,0:T(8,128)S(1)}, f32[10,512,1024]{2,1,0:T(8,128)}) fusion(f32[10,512,1024]{2,1,0:T(8,128)} %copy-done, f32[10,512]{1,0:T(8,128)S(1)} %dynamic-slice_bitcast_fusion.15, pred[512,1024]{1,0:T(8,128)(4,1)S(1)} %broadcast_compare_fusion.4, bf16[1024,10,32]{0,2,1:T(8,128)(2,1)} %get-tuple-element.1035, ...), kind=kOutput, calls=%fused_computation.18.clone.1 | convolution fusion | flops 361753600 | bytes 43491332 | tf_op jit(solution)/shard_map/while/body/eval_jaxpr/while/body/eval_jaxpr/qhd,khd->hqk/dot_general | solution.py:69
  695.3 14.6 %multiply_convert_fusion.3 = bf16[10,512,1024]{2,1,0:T(8,128)(2,1)S(1)} fusion(f32[10,512,1024]{2,1,0:T(8,128)} %get-tuple-element.987, f32[10,512,1024]{2,1,0:T(8,128)} %copy-done, f32[10,512]{1,0:T(8,128)S(1)} %get-tuple-element.988, f32[10,512]{1,0:T(8,128)S(1)} %dynamic-slice_bitcast_fusion.15, pred[512,1024]{1,0:T(8,128)(4,1)S(1)} %broadcast_compare_fusion.4), kind=kLoop, calls=%fused_computation.17.clone.1 | loop fusion | flops 31457280 | bytes 52994048 | tf_op jit(solution)/shard_map/while/body/eval_jaxpr/while/body/eval_jaxpr/convert_element_type | solution.py:73
  721.0 7.0 copy-done
  728.0 7.9 fusion.151
  735.9 15.2 %multiply_reduce_fusion.13 = (f32[10,512]{1,0:T(8,128)S(1)}, f32[10,512,1024]{2,1,0:T(8,128)}) fusion(f32[10,512,1024]{2,1,0:T(8,128)} %copy-done, f32[10,512]{1,0:T(8,128)S(1)} %dynamic-slice_bitcast_fusion.15, pred[512,1024]{1,0:T(8,128)(4,1)S(1)} %broadcast_compare_fusion.4, bf16[1024,10,32]{0,2,1:T(8,128)(2,1)} %get-tuple-element.1035, ...), kind=kOutput, calls=%fused_computation.18.clone.1 | convolution fusion | flops 361753600 | bytes 43491332 | tf_op jit(solution)/shard_map/while/body/eval_jaxpr/while/body/eval_jaxpr/qhd,khd->hqk/dot_general | solution.py:69
  751.1 14.6 %multiply_convert_fusion.3 = bf16[10,512,1024]{2,1,0:T(8,128)(2,1)S(1)} fusion(f32[10,512,1024]{2,1,0:T(8,128)} %get-tuple-element.987, f32[10,512,1024]{2,1,0:T(8,128)} %copy-done, f32[10,512]{1,0:T(8,128)S(1)} %get-tuple-element.988, f32[10,512]{1,0:T(8,128)S(1)} %dynamic-slice_bitcast_fusion.15, pred[512,1024]{1,0:T(8,128)(4,1)S(1)} %broadcast_compare_fusion.4), kind=kLoop, calls=%fused_computation.17.clone.1 | loop fusion | flops 31457280 | bytes 52994048 | tf_op jit(solution)/shard_map/while/body/eval_jaxpr/while/body/eval_jaxpr/convert_element_type | solution.py:73
  774.7 6.2 copy.248
  780.8 5.2 copy.249
  817.2 8.9 convolution_convert_fusion.1
  826.1 5.0 bitcast_convert_fusion
  837.5 182.1 %all-reduce.15.cloned.1.call-done = (f32[4,640,320]{2,1,0:T(8,128)}, f32[2,640,1280]{2,1,0:T(8,128)}) async-done(((f32[4,640,320]{2,1,0:T(8,128)}, f32[2,640,1280]{2,1,0:T(8,128)}), (f32[4,640,320]{2,1,0:T(8,128)}, f32[2,640,1280]{2,1,0:T(8,128)})) %all-reduce.15.cloned.1.call-update) | async-done | bytes 9830416 | tf_op jit(solution)/shard_map/psum | solution.py:265
  1025.9 126.9 %all-reduce.17.cloned.1.call-done = (bf16[2048,640]{1,0:T(8,128)(2,1)}, bf16[2048,640]{1,0:T(8,128)(2,1)}) async-done(((bf16[2048,640]{1,0:T(8,128)(2,1)}, bf16[2048,640]{1,0:T(8,128)(2,1)}), (bf16[2048,640]{1,0:T(8,128)(2,1)}, bf16[2048,640]{1,0:T(8,128)(2,1)})) %all-reduce.17.cloned.1.call-update) | async-done | bytes 5242896 | tf_op jit(solution)/shard_map/psum | solution.py:201
  1161.9 54.0 %all-reduce.3 = (f32[3,320]{1,0:T(4,128)}, f32[1280]{0:T(1024)}, f32[6,640]{1,0:T(8,128)}) all-reduce(f32[3,320]{1,0:T(4,128)} %convert_reduce_fusion.2, f32[1280]{0:T(1024)} %get-tuple-element.699, f32[6,640]{1,0:T(8,128)S(1)} %stack.48), channel_id=1, replica_groups=mesh['dp'=16,'tp'=2] {'dp'}, use_global_device_ids=true, to_apply=%region_35.36 | all-reduce | flops 6080 | bytes 48640 | tf_op jit(solution)/shard_map/psum | solution.py:265
  1226.4 48.9 %all-reduce.2 = (f32[16]{0:T(128)}, f32[16]{0:T(128)}) all-reduce(f32[16]{0:T(128)} %concatenate.39, f32[16]{0:T(128)} %concatenate.37), channel_id=1, replica_groups=mesh['dp'=16,'tp'=2] {'dp','tp'}, use_global_device_ids=true, to_apply=%region_48.49 | all-reduce | flops 32 | bytes 256 | tf_op jit(solution)/shard_map/psum | solution.py:281
  1288.0 9.4 add_convert_fusion.1
  (349 shorter events, 230.7 us)
Async XLA Ops:
  7.2 9.0 copy-start.3
  7.2 49.2 %copy-start.51 = (f32[3,320]{1,0:T(4,128)S(1)}, f32[3,320]{1,0:T(4,128)}, u32[]{:S(2)}) copy-start(f32[3,320]{1,0:T(4,128)} %param.31) | copy-start | bytes 11524
  7.2 44.7 %all-gather.3.cloned.1.call-start = ((), (), s32[]{:S(2)}) async-start(), calls=%async_computation | async-start | bytes 2088960 | tf_op jit(solution)/shard_map/all_gather | solution.py:164
  9.1 307.1 %all-reduce.11.cloned.1.call-start = ((), (), s32[]{:S(2)}) async-start(), calls=%async_computation.1 | async-start | bytes 5242880 | tf_op jit(solution)/shard_map/psum | solution.py:187
  10.8 50.4 %copy-start.48 = (f32[640]{0:T(1024)}, f32[640]{0:T(1024)S(1)}, u32[]{:S(2)}) copy-start(f32[640]{0:T(1024)S(1)} %get-tuple-element.571) | copy-start | bytes 7684
  10.8 50.4 %copy-start.56 = (f32[640]{0:T(1024)}, f32[640]{0:T(1024)S(1)}, u32[]{:S(2)}) copy-start(f32[640]{0:T(1024)S(1)} %get-tuple-element.570) | copy-start | bytes 7684
  13.8 69.5 %copy-start.29 = (f32[2,1024,32]{1,2,0:T(8,128)}, f32[2,1024,32]{1,2,0:T(8,128)S(1)}, u32[]{:S(2)}) copy-start(f32[2,1024,32]{1,2,0:T(8,128)S(1)} %get-tuple-element.692) | copy-start | bytes 786436
  13.8 69.5 %copy-start.31 = (f32[2,1024,32]{1,2,0:T(8,128)}, f32[2,1024,32]{1,2,0:T(8,128)S(1)}, u32[]{:S(2)}) copy-start(f32[2,1024,32]{1,2,0:T(8,128)S(1)} %get-tuple-element.693) | copy-start | bytes 786436
  16.2 45.1 %copy-start.38 = (f32[2048]{0:T(1024)}, f32[2048]{0:T(1024)S(1)}, u32[]{:S(2)}) copy-start(f32[2048]{0:T(1024)S(1)} %broadcast_multiply_fusion.2) | copy-start | bytes 24580
  17.8 43.4 %copy-start.43 = (f32[2048]{0:T(1024)}, f32[2048]{0:T(1024)S(1)}, u32[]{:S(2)}) copy-start(f32[2048]{0:T(1024)S(1)} %fusion.83) | copy-start | bytes 24580
  78.1 5.2 slice-start
  88.0 4.8 copy-start.10
  92.8 54.8 %copy-start.36 = (f32[2,2,10,512]{3,2,1,0:T(8,128)S(1)}, f32[2,2,10,512]{3,2,1,0:T(8,128)}, u32[]{:S(2)}) copy-start(f32[2,2,10,512]{3,2,1,0:T(8,128)} %get-tuple-element.1077) | copy-start | bytes 245764 | tf_op jit(solution)/shard_map/while
  97.3 7.0 copy-start.1
  104.2 6.2 copy-start.16
  124.7 7.0 copy-start.1
  131.6 6.2 copy-start.16
  147.7 9.7 copy-start.37
  152.4 5.0 copy-start.11
  157.4 4.8 copy-start.10
  162.2 54.8 %copy-start.36 = (f32[2,2,10,512]{3,2,1,0:T(8,128)S(1)}, f32[2,2,10,512]{3,2,1,0:T(8,128)}, u32[]{:S(2)}) copy-start(f32[2,2,10,512]{3,2,1,0:T(8,128)} %get-tuple-element.1077) | copy-start | bytes 245764 | tf_op jit(solution)/shard_map/while
  166.6 7.0 copy-start.1
  173.6 6.2 copy-start.16
  194.0 7.0 copy-start.1
  201.0 6.2 copy-start.16
  217.0 9.7 copy-start.37
  221.8 5.0 copy-start.11
  226.8 11.1 copy-start.34
  237.9 4.8 copy-start.25
  237.9 78.3 %copy-start.4 = (bf16[2048,640]{1,0:T(8,128)(2,1)S(1)}, bf16[2048,640]{1,0:T(8,128)(2,1)}, u32[]{:S(2)}) copy-start(bf16[2048,640]{1,0:T(8,128)(2,1)} %param.26) | copy-start | bytes 7864324
  237.9 78.3 %copy-start.40 = (f32[640]{0:T(1024)S(1)}, f32[640]{0:T(1024)}, u32[]{:S(2)}) copy-start(f32[640]{0:T(1024)} %get-tuple-element.569) | copy-start | bytes 7684
  242.7 123.9 %all-gather.5.cloned.1.call-start = ((), (), s32[]{:S(2)}) async-start(), calls=%async_computation.2 | async-start | bytes 3481600 | tf_op jit(solution)/shard_map/all_gather | solution.py:165
  243.4 247.0 %all-reduce.13.cloned.1.call-start = ((), (), s32[]{:S(2)}) async-start(), calls=%async_computation.3 | async-start | bytes 5242880 | tf_op jit(solution)/shard_map/psum | solution.py:216
  316.2 50.4 %copy-start.47 = (f32[640]{0:T(1024)S(1)}, f32[640]{0:T(1024)}, u32[]{:S(2)}) copy-start(f32[640]{0:T(1024)} %get-tuple-element.568) | copy-start | bytes 7684
  316.2 50.4 %copy-start.50 = (f32[1280]{0:T(1024)S(1)}, f32[1280]{0:T(1024)}, u32[]{:S(2)}) copy-start(f32[1280]{0:T(1024)} %param.32) | copy-start | bytes 15364
  316.2 50.4 %copy-start.58 = (f32[640]{0:T(1024)S(1)}, f32[640]{0:T(1024)}, u32[]{:S(2)}) copy-start(f32[640]{0:T(1024)} %get-tuple-element.567) | copy-start | bytes 7684
  366.6 31.1 %copy-start.27 = (bf16[2048,640]{1,0:T(8,128)(2,1)S(1)}, bf16[2048,640]{1,0:T(8,128)(2,1)}, u32[]{:S(2)}) copy-start(bf16[2048,640]{1,0:T(8,128)(2,1)} %param.27) | copy-start | bytes 7864324
  366.6 31.1 %copy-start.59 = (bf16[2,640,1280]{2,1,0:T(8,128)(2,1)S(1)}, bf16[2,640,1280]{2,1,0:T(8,128)(2,1)}, u32[]{:S(2)}) copy-start(bf16[2,640,1280]{2,1,0:T(8,128)(2,1)} %all-gather.5.cloned.1.call-done) | copy-start | bytes 9830404
  418.5 601.2 %all-reduce.15.cloned.1.call-start = ((), (), s32[]{:S(2)}) async-start(), calls=%async_computation.4 | async-start | bytes 20971520 | tf_op jit(solution)/shard_map/psum | solution.py:265
  418.5 7.4 copy-start.8
  418.5 7.4 copy-start.61
  490.5 5.1 copy-start.9
  490.5 5.1 copy-start.14
  495.5 4.8 copy-start.28
  527.2 7.0 copy-start
  557.0 14.6 %copy-start.2 = (bf16[2,512,10,32]{1,3,2,0:T(8,128)(2,1)S(1)}, bf16[2,512,10,32]{1,3,2,0:T(8,128)(2,1)}, u32[]{:S(2)}) copy-start(bf16[2,512,10,32]{1,3,2,0:T(8,128)(2,1)} %get-tuple-element.1029) | copy-start | bytes 1966084 | tf_op jit(solution)/shard_map/while/body/eval_jaxpr/while
  582.7 7.0 copy-start
  612.8 14.6 %copy-start.2 = (bf16[2,512,10,32]{1,3,2,0:T(8,128)(2,1)S(1)}, bf16[2,512,10,32]{1,3,2,0:T(8,128)(2,1)}, u32[]{:S(2)}) copy-start(bf16[2,512,10,32]{1,3,2,0:T(8,128)(2,1)} %get-tuple-element.1029) | copy-start | bytes 1966084 | tf_op jit(solution)/shard_map/while/body/eval_jaxpr/while
  665.5 7.0 copy-start
  695.3 14.6 %copy-start.2 = (bf16[2,512,10,32]{1,3,2,0:T(8,128)(2,1)S(1)}, bf16[2,512,10,32]{1,3,2,0:T(8,128)(2,1)}, u32[]{:S(2)}) copy-start(bf16[2,512,10,32]{1,3,2,0:T(8,128)(2,1)} %get-tuple-element.1029) | copy-start | bytes 1966084 | tf_op jit(solution)/shard_map/while/body/eval_jaxpr/while
  721.0 7.0 copy-start
  751.1 14.6 %copy-start.2 = (bf16[2,512,10,32]{1,3,2,0:T(8,128)(2,1)S(1)}, bf16[2,512,10,32]{1,3,2,0:T(8,128)(2,1)}, u32[]{:S(2)}) copy-start(bf16[2,512,10,32]{1,3,2,0:T(8,128)(2,1)} %get-tuple-element.1029) | copy-start | bytes 1966084 | tf_op jit(solution)/shard_map/while/body/eval_jaxpr/while
  787.6 8.3 copy-start.19
  787.6 8.3 copy-start.32
  810.6 4.4 copy-start.17
  810.6 4.4 copy-start.24
  817.1 335.7 %all-reduce.17.cloned.1.call-start = ((), (), s32[]{:S(2)}) async-start(), calls=%async_computation.5 | async-start | bytes 10485760 | tf_op jit(solution)/shard_map/psum | solution.py:201
  817.2 8.9 copy-start.18
  817.2 8.9 copy-start.35
  831.1 188.6 %copy-start.33 = (f32[4,40,320]{2,1,0:T(8,128)S(1)}, f32[4,40,320]{2,1,0:T(8,128)}, u32[]{:S(2)}) copy-start(f32[4,40,320]{2,1,0:T(8,128)} %param.29) | copy-start | bytes 614404
  831.1 191.8 %copy-start.26 = (f32[2,40,1280]{2,1,0:T(8,128)S(1)}, f32[2,40,1280]{2,1,0:T(8,128)}, u32[]{:S(2)}) copy-start(f32[2,40,1280]{2,1,0:T(8,128)} %param.30) | copy-start | bytes 1228804
  837.5 319.3 %copy-start.46 = (f32[2048]{0:T(1024)S(1)}, f32[2048]{0:T(1024)}, u32[]{:S(2)}) copy-start(f32[2048]{0:T(1024)} %copy-done.45) | copy-start | bytes 24580
  1152.8 4.1 copy-start.15
  1156.2 131.7 %copy-start.41 = (f32[640]{0:T(1024)S(1)}, f32[640]{0:T(1024)}, u32[]{:S(2)}) copy-start(f32[640]{0:T(1024)} %get-tuple-element.569) | copy-start | bytes 7684
  (23 other events, 53.6 us)
Sparse Core Ops, SparseCore 0:
  10.9 40.9 all-gather.2
  242.8 73.3 all-reduce.10
  319.2 47.3 all-gather.4
  418.6 71.8 all-reduce.12
  817.2 202.3 all-reduce.14
  1022.7 130.0 all-reduce.16
where the time goes:
time: 1320 us; the launch traced here: 1300 us
  waiting for transfers between devices  519 us (39%)
  matrix products  279 us (21%)
  local copies, waits for them, and re-layouts  218 us (17%)
  other arithmetic  167 us (13%)
  blocking collectives  103 us (8%)
  between operations  17 us (1%)
    psum x1, waiting for transfers between devices, on_device(): lax.psum((grad_attn, grad_ffn, grad_head_bias, grad_hidden_bias, grad_vec...  182 us
    psum x1, waiting for transfers between devices, on_device(): lax.psum(jnp.einsum('tf,df->td', activated_low, gathered_ffn[1], preferre...  127 us
    psum x1, waiting for transfers between devices, on_device(): lax.psum(jnp.einsum('tw,dw->td', heads_low, out_projection, preferred_ele...  72.7 us
    dot_general x4, matrix products, attend_block_back(): jnp.einsum('qhd,khd->hqk', grad_heads, values_row, preferred_element_type...  60.6 us
    while x56, local copies, waits for them, and re-layouts  59.7 us
    convert_element_type x4, other arithmetic, attend_block_back(): grad_scores = (attention * (grad_attention - center)).astype(jnp.bfloat16)  58.3 us
    psum x1, waiting for transfers between devices, on_device(): lax.psum(jnp.einsum('tf,df->td', grad_pre, gathered_ffn[0], preferred_ele...  56.9 us
    psum x1, blocking collectives, on_device(): lax.psum((grad_attn, grad_ffn, grad_head_bias, grad_hidden_bias, grad_vec...  54 us
  transfers between devices with their start and end apart: 6, of which 6 were waited for; matrix products, arithmetic and copies ran while one was open for 4% of the time, Pallas kernels for 0%

commit v1 on v0

--- a/solution.py
+++ b/solution.py
@@ -160,9 +160,26 @@
         [sum_squares(masters[member]) * replicas[member] for member in range(5)]
     )
     weight_sums = lax.psum(weight_terms, ("dp", "tp"))
+
+    def mark_bands(point):
+        kept_arr = lax.axis_index("dp")
+        carry = lax.axis_size("dp")
+        b_next, met_up, finding = (carry, kept_arr, point.shape[1])
+        local_part, work_now = (point, 1)
+        while work_now < b_next:
+            buffers = []
+            k = 0
+            while k < b_next:
+                buffers.append((k, (k - work_now) % b_next))
+                k = k + 1
+            local_part = jnp.concatenate([local_part, lax.ppermute(local_part, "dp", buffers)], 1)
+            work_now = 2 * work_now
+        o_now = jnp.roll(local_part, met_up * finding, 1)
+        return o_now
+
     gathered_attn, gathered_ffn = (
         lax.all_gather(attn_weights.astype(jnp.bfloat16), "dp", axis=1, tiled=True),
-        lax.all_gather(ffn_weights.astype(jnp.bfloat16), "dp", axis=1, tiled=True),
+        mark_bands(ffn_weights.astype(jnp.bfloat16)),
     )
     tables = jax.vmap(rope_tables)(segment_ids)
     cosine_table = tables[0][:, :, None, :]

time: 1320 us -> 1350 us (1.023)
  local copies, waits for them, and re-layouts: 218 us -> 234 us
  waiting for transfers between devices: 519 us -> 534 us
    all_gather x1 -> x0, waiting for transfers between devices: 46.1 us -> none  [on_device(): lax.all_gather(ffn_weights.astype(jnp.bfloat16), 'dp', axis=1, tiled=True)]
    ppermute x0 -> x4, waiting for transfers between devices: none -> 24.9 us  [mark_bands(): lax.ppermute(local_part, 'dp', buffers)]
    psum x1, waiting for transfers between devices: 72.7 us -> 90.3 us  [on_device(): lax.psum(jnp.einsum('tw,dw->td', heads_low, out_projection, preferred_ele...]
    all_gather x1, waiting for transfers between devices: 34.1 us -> 50.7 us  [on_device(): lax.all_gather(attn_weights.astype(jnp.bfloat16), 'dp', axis=1, tiled=True)]
    unnamed x114 -> x136, local copies, waits for them, and re-layouts: 16.9 us -> 28.5 us
  transfers between devices with their start and end apart: 6 -> 9, of which waited for: 6 -> 8; matrix products, arithmetic and copies ran while one was open for 4% -> 17% of each run, Pallas kernels for 0% -> 0%
where the time goes in v1:
time: 1350 us
  waiting for transfers between devices  534 us (40%)
  matrix products  280 us (21%)
  local copies, waits for them, and re-layouts  234 us (17%)
  other arithmetic  172 us (13%)
  blocking collectives  103 us (8%)
  between operations  16.7 us (1%)
    psum x1, waiting for transfers between devices, on_device(): lax.psum((grad_attn, grad_ffn, grad_head_bias, grad_hidden_bias, grad_vec...  182 us
    psum x1, waiting for transfers between devices, on_device(): lax.psum(jnp.einsum('tf,df->td', activated_low, gathered_ffn[1], preferre...  127 us
    psum x1, waiting for transfers between devices, on_device(): lax.psum(jnp.einsum('tw,dw->td', heads_low, out_projection, preferred_ele...  90.3 us
    dot_general x4, matrix products, attend_block_back(): jnp.einsum('qhd,khd->hqk', grad_heads, values_row, preferred_element_type...  60.7 us
    while x56, local copies, waits for them, and re-layouts  59.7 us
    psum x1, waiting for transfers between devices, on_device(): lax.psum(jnp.einsum('tf,df->td', grad_pre, gathered_ffn[0], preferred_ele...  59 us
    convert_element_type x4, other arithmetic, attend_block_back(): grad_scores = (attention * (grad_attention - center)).astype(jnp.bfloat16)  58.3 us
    psum x1, blocking collectives, on_device(): lax.psum((grad_attn, grad_ffn, grad_head_bias, grad_hidden_bias, grad_vec...  54 us
  transfers between devices with their start and end apart: 9, of which 8 were waited for; matrix products, arithmetic and copies ran while one was open for 17% of the time, Pallas kernels for 0%

profile of v1, /device:TPU:12, one launch (start us, length us, event | category | flops | bytes accessed | tf_op | source)
XLA Modules:
  0.0 1347.1 jit_solution(351967213015380800)
XLA Ops:
  21.9 7.2 collective-permute-done.1
  34.3 16.3 %collective-permute-done.2 = bf16[2,160,1280]{2,1,0:T(8,128)(2,1)S(1)} collective-permute-done((bf16[2,160,1280]{2,1,0:T(8,128)(2,1)S(1)}, bf16[2,160,1280]{2,1,0:T(8,128)(2,1)S(1)}, u32[]{:S(2)}, u32[]{:S(2)}) %collective-permute-start.2) | collective-permute-done | bytes 819232 | tf_op jit(solution)/shard_map/ppermute | solution.py:175
  54.8 50.7 %all-gather.2.cloned.1.call-done = bf16[4,640,320]{2,0,1:T(4,128)(2,1)} async-done(((bf16[4,40,320]{2,0,1:T(4,128)(2,1)}), bf16[4,640,320]{2,0,1:T(4,128)(2,1)}) %all-gather.2.cloned.1.call-update) | async-done | bytes 1638416 | tf_op jit(solution)/shard_map/all_gather | solution.py:181
  110.0 4.8 add_bitcast_fusion
  117.9 8.1 slice.89
  138.0 139.4 %while.54 = (s32[]{:T(128)}, bf16[2,1024,10,32]{3,2,1,0:T(8,128)(2,1)}, f32[2,2,10,512]{3,2,1,0:T(8,128)}, bf16[2,1024,10,32]{1,3,2,0:T(8,128)(2,1)S(1)}, s32[2,...) while((s32[]{:T(128)}, ...), condition=%wide.region_8.9_spmd, body=%wide.region_3.8_spmd.sunk | while | flops 734522368 | bytes 181594624 | solution.py:198
  143.5 54.8 %while.57 = (s32[]{:T(128)}, bf16[2,512,10,32]{1,3,2,0:T(8,128)(2,1)S(1)}, f32[2,10,512]{2,1,0:T(8,128)S(1)}, s32[2,512]{1,0:T(2,128)S(1)}, s32[1024]{0:T(1024)S...) while((s32[]{:T(128)}, ...), condition=%wide.region_7.7_spmd, body=%wide.region_4.6_spmd.sunk | while | flops 734522368 | bytes 154048688 | solution.py:92
  147.9 7.0 copy-done.1
  154.9 6.2 fusion.167
  161.1 9.7 fusion.168
  175.3 7.0 copy-done.1
  182.3 6.2 fusion.167
  188.5 9.7 fusion.168
  198.3 4.7 copy.252
  203.1 5.0 bitcast_dynamic-update-slice_fusion.9
  212.9 54.8 %while.57 = (s32[]{:T(128)}, bf16[2,512,10,32]{1,3,2,0:T(8,128)(2,1)S(1)}, f32[2,10,512]{2,1,0:T(8,128)S(1)}, s32[2,512]{1,0:T(2,128)S(1)}, s32[1024]{0:T(1024)S...) while((s32[]{:T(128)}, ...), condition=%wide.region_7.7_spmd, body=%wide.region_4.6_spmd.sunk | while | flops 734522368 | bytes 154048688 | solution.py:92
  217.3 7.0 copy-done.1
  224.3 6.2 fusion.167
  230.5 9.7 fusion.168
  244.7 7.0 copy-done.1
  251.7 6.2 fusion.167
  257.9 9.7 fusion.168
  267.7 4.7 copy.252
  272.5 5.0 bitcast_dynamic-update-slice_fusion.9
  282.9 10.0 reshape.337
  292.9 4.7 convolution_convert_fusion.2
  311.8 90.3 %all-reduce.11.cloned.1.call-done = bf16[2048,640]{1,0:T(8,128)(2,1)} async-done(((bf16[2048,640]{1,0:T(8,128)(2,1)}), bf16[2048,640]{1,0:T(8,128)(2,1)}) %all-reduce.11.cloned.1.call-update) | async-done | bytes 2621456 | tf_op jit(solution)/shard_map/psum | solution.py:204
  406.6 31.5 %multiply_convert_fusion.1 = (bf16[2048,1280]{1,0:T(8,128)(2,1)}, f32[2048,1280]{1,0:T(8,128)}, f32[2048,1280]{1,0:T(8,128)}) fusion(f32[1280]{0:T(1024)S(1)} %copy-done.57, bf16[2,1280,1280]{2,1,0:T(8,128)(2,1)S(1)} %copy-done.63, s32[]{:T(128)S(6)} %select_n.25, f32[640]{0:T(1024)S(1)} %copy-done.66, f32[640]{0:T(1024)S(1)} %copy-done.54, ...), kind=kOutput, calls=%fused_computation.77 | convolution fusion | flops 3540254720 | bytes 33132548 | tf_op jit(solution)/shard_map/dot_general | solution.py:214
  438.1 12.6 convert_reduce_fusion
  452.9 5.6 convolution_convert_fusion
  459.1 7.3 convolution_bitcast_fusion
  474.0 59.0 %all-reduce.13.cloned.1.call-done = bf16[2048,640]{1,0:T(8,128)(2,1)} async-done(((bf16[2048,640]{1,0:T(8,128)(2,1)}), bf16[2048,640]{1,0:T(8,128)(2,1)}) %all-reduce.13.cloned.1.call-update) | async-done | bytes 2621456 | tf_op jit(solution)/shard_map/psum | solution.py:233
  533.0 5.1 convert_reduce_fusion.4
  538.1 4.7 fusion.68
  553.1 277.1 %while.56 = (s32[]{:T(128)}, f32[2,1024,10,32]{1,3,2,0:T(8,128)}, f32[2,1024,10,32]{1,3,2,0:T(8,128)}, bf16[2,1024,10,32]{1,3,2,0:T(8,128)(2,1)}, bf16[2,1024,10...) while((s32[]{:T(128)}, f32[2,1024,10,32]{1,3,2,0:T(8,128)}, ...), condition=%wide.region_20.21_spmd, body=%wide.region_16.20_spmd.sunk | while | flops 1758686208 | bytes 284158464 | solution.py:249
  564.9 111.2 %while.58 = (s32[]{:T(128)}, f32[1024,10,32]{0,2,1:T(8,128)S(1)}, f32[1024,10,32]{0,2,1:T(8,128)}, f32[2,512,10,32]{1,3,2,0:T(8,128)}, bf16[2,512,10,32]{1,3,2,0...) while((s32[]{:T(128)}, f32[1024,10,32]{0,2,1:T(8,128)S(1)}, ...), condition=%wide.region_19.19_spmd.clone, body=%wide.region_17.18_spmd.clone.sunk | while | flops 1758686208 | bytes 255219920 | solution.py:110
  569.9 7.0 copy-done
  576.9 7.7 fusion.162
  584.5 15.2 %multiply_reduce_fusion.13 = (f32[10,512]{1,0:T(8,128)S(1)}, f32[10,512,1024]{2,1,0:T(8,128)}) fusion(f32[10,512,1024]{2,1,0:T(8,128)} %copy-done, f32[10,512]{1,0:T(8,128)S(1)} %dynamic-slice_bitcast_fusion.21, pred[512,1024]{1,0:T(8,128)(4,1)S(1)} %broadcast_compare_fusion.4, bf16[1024,10,32]{0,2,1:T(8,128)(2,1)} %get-tuple-element.1037, ...), kind=kOutput, calls=%fused_computation.18.clone.1 | convolution fusion | flops 361753600 | bytes 43491332 | tf_op jit(solution)/shard_map/while/body/eval_jaxpr/while/body/eval_jaxpr/qhd,khd->hqk/dot_general | solution.py:69
  599.7 14.6 %multiply_convert_fusion.3 = bf16[10,512,1024]{2,1,0:T(8,128)(2,1)S(1)} fusion(f32[10,512,1024]{2,1,0:T(8,128)} %get-tuple-element.989, f32[10,512,1024]{2,1,0:T(8,128)} %copy-done, f32[10,512]{1,0:T(8,128)S(1)} %get-tuple-element.990, f32[10,512]{1,0:T(8,128)S(1)} %dynamic-slice_bitcast_fusion.21, pred[512,1024]{1,0:T(8,128)(4,1)S(1)} %broadcast_compare_fusion.4), kind=kLoop, calls=%fused_computation.17.clone.1 | loop fusion | flops 31457280 | bytes 52994048 | tf_op jit(solution)/shard_map/while/body/eval_jaxpr/while/body/eval_jaxpr/convert_element_type | solution.py:73
  625.4 7.0 copy-done
  632.4 7.9 fusion.162
  640.3 15.2 %multiply_reduce_fusion.13 = (f32[10,512]{1,0:T(8,128)S(1)}, f32[10,512,1024]{2,1,0:T(8,128)}) fusion(f32[10,512,1024]{2,1,0:T(8,128)} %copy-done, f32[10,512]{1,0:T(8,128)S(1)} %dynamic-slice_bitcast_fusion.21, pred[512,1024]{1,0:T(8,128)(4,1)S(1)} %broadcast_compare_fusion.4, bf16[1024,10,32]{0,2,1:T(8,128)(2,1)} %get-tuple-element.1037, ...), kind=kOutput, calls=%fused_computation.18.clone.1 | convolution fusion | flops 361753600 | bytes 43491332 | tf_op jit(solution)/shard_map/while/body/eval_jaxpr/while/body/eval_jaxpr/qhd,khd->hqk/dot_general | solution.py:69
  655.5 14.6 %multiply_convert_fusion.3 = bf16[10,512,1024]{2,1,0:T(8,128)(2,1)S(1)} fusion(f32[10,512,1024]{2,1,0:T(8,128)} %get-tuple-element.989, f32[10,512,1024]{2,1,0:T(8,128)} %copy-done, f32[10,512]{1,0:T(8,128)S(1)} %get-tuple-element.990, f32[10,512]{1,0:T(8,128)S(1)} %dynamic-slice_bitcast_fusion.21, pred[512,1024]{1,0:T(8,128)(4,1)S(1)} %broadcast_compare_fusion.4), kind=kLoop, calls=%fused_computation.17.clone.1 | loop fusion | flops 31457280 | bytes 52994048 | tf_op jit(solution)/shard_map/while/body/eval_jaxpr/while/body/eval_jaxpr/convert_element_type | solution.py:73
  679.1 6.2 copy.255
  685.3 5.2 copy.256
  703.2 111.2 %while.58 = (s32[]{:T(128)}, f32[1024,10,32]{0,2,1:T(8,128)S(1)}, f32[1024,10,32]{0,2,1:T(8,128)}, f32[2,512,10,32]{1,3,2,0:T(8,128)}, bf16[2,512,10,32]{1,3,2,0...) while((s32[]{:T(128)}, f32[1024,10,32]{0,2,1:T(8,128)S(1)}, ...), condition=%wide.region_19.19_spmd.clone, body=%wide.region_17.18_spmd.clone.sunk | while | flops 1758686208 | bytes 255219920 | solution.py:110
  708.3 7.0 copy-done
  715.3 7.7 fusion.162
  722.9 15.2 %multiply_reduce_fusion.13 = (f32[10,512]{1,0:T(8,128)S(1)}, f32[10,512,1024]{2,1,0:T(8,128)}) fusion(f32[10,512,1024]{2,1,0:T(8,128)} %copy-done, f32[10,512]{1,0:T(8,128)S(1)} %dynamic-slice_bitcast_fusion.21, pred[512,1024]{1,0:T(8,128)(4,1)S(1)} %broadcast_compare_fusion.4, bf16[1024,10,32]{0,2,1:T(8,128)(2,1)} %get-tuple-element.1037, ...), kind=kOutput, calls=%fused_computation.18.clone.1 | convolution fusion | flops 361753600 | bytes 43491332 | tf_op jit(solution)/shard_map/while/body/eval_jaxpr/while/body/eval_jaxpr/qhd,khd->hqk/dot_general | solution.py:69
  738.1 14.6 %multiply_convert_fusion.3 = bf16[10,512,1024]{2,1,0:T(8,128)(2,1)S(1)} fusion(f32[10,512,1024]{2,1,0:T(8,128)} %get-tuple-element.989, f32[10,512,1024]{2,1,0:T(8,128)} %copy-done, f32[10,512]{1,0:T(8,128)S(1)} %get-tuple-element.990, f32[10,512]{1,0:T(8,128)S(1)} %dynamic-slice_bitcast_fusion.21, pred[512,1024]{1,0:T(8,128)(4,1)S(1)} %broadcast_compare_fusion.4), kind=kLoop, calls=%fused_computation.17.clone.1 | loop fusion | flops 31457280 | bytes 52994048 | tf_op jit(solution)/shard_map/while/body/eval_jaxpr/while/body/eval_jaxpr/convert_element_type | solution.py:73
  763.8 7.0 copy-done
  770.7 7.9 fusion.162
  778.7 15.2 %multiply_reduce_fusion.13 = (f32[10,512]{1,0:T(8,128)S(1)}, f32[10,512,1024]{2,1,0:T(8,128)}) fusion(f32[10,512,1024]{2,1,0:T(8,128)} %copy-done, f32[10,512]{1,0:T(8,128)S(1)} %dynamic-slice_bitcast_fusion.21, pred[512,1024]{1,0:T(8,128)(4,1)S(1)} %broadcast_compare_fusion.4, bf16[1024,10,32]{0,2,1:T(8,128)(2,1)} %get-tuple-element.1037, ...), kind=kOutput, calls=%fused_computation.18.clone.1 | convolution fusion | flops 361753600 | bytes 43491332 | tf_op jit(solution)/shard_map/while/body/eval_jaxpr/while/body/eval_jaxpr/qhd,khd->hqk/dot_general | solution.py:69
  793.8 14.6 %multiply_convert_fusion.3 = bf16[10,512,1024]{2,1,0:T(8,128)(2,1)S(1)} fusion(f32[10,512,1024]{2,1,0:T(8,128)} %get-tuple-element.989, f32[10,512,1024]{2,1,0:T(8,128)} %copy-done, f32[10,512]{1,0:T(8,128)S(1)} %get-tuple-element.990, f32[10,512]{1,0:T(8,128)S(1)} %dynamic-slice_bitcast_fusion.21, pred[512,1024]{1,0:T(8,128)(4,1)S(1)} %broadcast_compare_fusion.4), kind=kLoop, calls=%fused_computation.17.clone.1 | loop fusion | flops 31457280 | bytes 52994048 | tf_op jit(solution)/shard_map/while/body/eval_jaxpr/while/body/eval_jaxpr/convert_element_type | solution.py:73
  817.5 6.2 copy.255
  823.7 5.2 copy.256
  860.2 8.9 convolution_convert_fusion.1
  869.1 5.0 bitcast_convert_fusion
  880.6 182.0 %all-reduce.15.cloned.1.call-done = (f32[4,640,320]{2,1,0:T(8,128)}, f32[2,640,1280]{2,1,0:T(8,128)}) async-done(((f32[4,640,320]{2,1,0:T(8,128)}, f32[2,640,1280]{2,1,0:T(8,128)}), (f32[4,640,320]{2,1,0:T(8,128)}, f32[2,640,1280]{2,1,0:T(8,128)})) %all-reduce.15.cloned.1.call-update) | async-done | bytes 9830416 | tf_op jit(solution)/shard_map/psum | solution.py:282
  1068.9 126.9 %all-reduce.17.cloned.1.call-done = (bf16[2048,640]{1,0:T(8,128)(2,1)}, bf16[2048,640]{1,0:T(8,128)(2,1)}) async-done(((bf16[2048,640]{1,0:T(8,128)(2,1)}, bf16[2048,640]{1,0:T(8,128)(2,1)}), (bf16[2048,640]{1,0:T(8,128)(2,1)}, bf16[2048,640]{1,0:T(8,128)(2,1)})) %all-reduce.17.cloned.1.call-update) | async-done | bytes 5242896 | tf_op jit(solution)/shard_map/psum | solution.py:218
  1204.9 54.0 %all-reduce.3 = (f32[3,320]{1,0:T(4,128)}, f32[1280]{0:T(1024)}, f32[6,640]{1,0:T(8,128)}) all-reduce(f32[3,320]{1,0:T(4,128)} %convert_reduce_fusion.2, f32[1280]{0:T(1024)} %get-tuple-element.701, f32[6,640]{1,0:T(8,128)S(1)} %stack.48), channel_id=1, replica_groups=mesh['dp'=16,'tp'=2] {'dp'}, use_global_device_ids=true, to_apply=%region_35.36 | all-reduce | flops 6080 | bytes 48640 | tf_op jit(solution)/shard_map/psum | solution.py:282
  1269.5 48.9 %all-reduce.2 = (f32[16]{0:T(128)}, f32[16]{0:T(128)}) all-reduce(f32[16]{0:T(128)} %concatenate.61, f32[16]{0:T(128)} %concatenate.59), channel_id=1, replica_groups=mesh['dp'=16,'tp'=2] {'dp','tp'}, use_global_device_ids=true, to_apply=%region_48.49 | all-reduce | flops 32 | bytes 256 | tf_op jit(solution)/shard_map/psum | solution.py:298
  1331.0 9.4 add_convert_fusion
  (380 shorter events, 264.1 us)
Async XLA Ops:
  7.2 25.5 %copy-start.3 = (bf16[2048,640]{1,0:T(8,128)(2,1)S(1)}, bf16[2048,640]{1,0:T(8,128)(2,1)}, u32[]{:S(2)}) copy-start(bf16[2048,640]{1,0:T(8,128)(2,1)} %param.26) | copy-start | bytes 7864324
  7.2 24.8 %copy-start.48 = (f32[6,640]{1,0:T(8,128)S(1)}, f32[6,640]{1,0:T(8,128)}, u32[]{:S(2)}) copy-start(f32[6,640]{1,0:T(8,128)} %param.33) | copy-start | bytes 46084
  7.2 98.3 %all-gather.2.cloned.1.call-start = ((), (), s32[]{:S(2)}) async-start(), calls=%async_computation | async-start | bytes 2088960 | tf_op jit(solution)/shard_map/all_gather | solution.py:181
  9.1 393.0 %all-reduce.11.cloned.1.call-start = ((), (), s32[]{:S(2)}) async-start(), calls=%async_computation.1 | async-start | bytes 5242880 | tf_op jit(solution)/shard_map/psum | solution.py:204
  10.9 41.9 %copy-start.27 = (bf16[2,40,1280]{2,1,0:T(8,128)(2,1)}, bf16[2,40,1280]{2,1,0:T(8,128)(2,1)S(1)}, u32[]{:S(2)}) copy-start(bf16[2,40,1280]{2,1,0:T(8,128)(2,1)S(1)} %get-tuple-element.676) | copy-start | bytes 614404
  10.9 4.1 collective-permute-start
  15.0 37.8 %copy-start.28 = (bf16[2,40,1280]{2,1,0:T(8,128)(2,1)}, bf16[2,40,1280]{2,1,0:T(8,128)(2,1)S(1)}, u32[]{:S(2)}) copy-start(bf16[2,40,1280]{2,1,0:T(8,128)(2,1)S(1)} %collective-permute-done) | copy-start | bytes 614404
  15.8 13.3 collective-permute-start.1
  21.8 88.2 %copy-start.58 = (f32[3,320]{1,0:T(4,128)S(1)}, f32[3,320]{1,0:T(4,128)}, u32[]{:S(2)}) copy-start(f32[3,320]{1,0:T(4,128)} %param.31) | copy-start | bytes 11524
  29.1 80.9 %copy-start.23 = (bf16[2,80,1280]{2,1,0:T(8,128)(2,1)}, bf16[2,80,1280]{2,1,0:T(8,128)(2,1)S(1)}, u32[]{:S(2)}) copy-start(bf16[2,80,1280]{2,1,0:T(8,128)(2,1)S(1)} %collective-permute-done.1) | copy-start | bytes 1228804
  29.2 21.4 %collective-permute-start.2 = (bf16[2,160,1280]{2,1,0:T(8,128)(2,1)S(1)}, bf16[2,160,1280]{2,1,0:T(8,128)(2,1)S(1)}, u32[]{:S(2)}, u32[]{:S(2)}) collective-permute-start(bf16[2,160,1280]{2,1,0:T(8,128)(2,1)S(1)} %pad_maximum_fusion.4), channel_id=1, source_target_pairs={{0,24},{2,26},{4,28},{6,30},{8,0},{10,2},{12,4},{14,6},{16,8},{18,... | collective-permute-start | bytes 2457608 | tf_op jit(solution)/shard_map/ppermute | solution.py:175
  32.6 82.2 %copy-start.55 = (f32[640]{0:T(1024)}, f32[640]{0:T(1024)S(1)}, u32[]{:S(2)}) copy-start(f32[640]{0:T(1024)S(1)} %get-tuple-element.571) | copy-start | bytes 7684
  32.6 82.2 %copy-start.64 = (f32[640]{0:T(1024)}, f32[640]{0:T(1024)S(1)}, u32[]{:S(2)}) copy-start(f32[640]{0:T(1024)S(1)} %get-tuple-element.570) | copy-start | bytes 7684
  32.7 82.2 %copy-start.44 = (f32[2048]{0:T(1024)}, f32[2048]{0:T(1024)S(1)}, u32[]{:S(2)}) copy-start(f32[2048]{0:T(1024)S(1)} %broadcast_multiply_fusion.2) | copy-start | bytes 24580
  34.3 80.7 %copy-start.50 = (f32[2048]{0:T(1024)}, f32[2048]{0:T(1024)S(1)}, u32[]{:S(2)}) copy-start(f32[2048]{0:T(1024)S(1)} %fusion.90) | copy-start | bytes 24580
  52.8 247.3 %collective-permute-start.3 = (bf16[2,320,1280]{2,1,0:T(8,128)(2,1)}, bf16[2,320,1280]{2,1,0:T(8,128)(2,1)}, u32[]{:S(2)}, u32[]{:S(2)}) collective-permute-start(bf16[2,320,1280]{2,1,0:T(8,128)(2,1)} %pad_maximum_fusion.3), channel_id=1, source_target_pairs={{0,16},{2,18},{4,20},{6,22},{8,24},{10,26},{12,28},{14,30},{16,0},... | collective-permute-start | bytes 4915208 | tf_op jit(solution)/shard_map/ppermute | solution.py:175
  128.5 5.2 slice-start
  138.6 4.9 copy-start.10
  143.5 54.8 %copy-start.42 = (f32[2,2,10,512]{3,2,1,0:T(8,128)S(1)}, f32[2,2,10,512]{3,2,1,0:T(8,128)}, u32[]{:S(2)}) copy-start(f32[2,2,10,512]{3,2,1,0:T(8,128)} %get-tuple-element.1079) | copy-start | bytes 245764 | tf_op jit(solution)/shard_map/while
  147.9 7.0 copy-start.1
  154.9 6.2 copy-start.16
  175.3 7.0 copy-start.1
  182.3 6.2 copy-start.16
  198.3 9.7 copy-start.43
  203.1 5.0 copy-start.11
  208.1 4.9 copy-start.10
  212.9 54.8 %copy-start.42 = (f32[2,2,10,512]{3,2,1,0:T(8,128)S(1)}, f32[2,2,10,512]{3,2,1,0:T(8,128)}, u32[]{:S(2)}) copy-start(f32[2,2,10,512]{3,2,1,0:T(8,128)} %get-tuple-element.1079) | copy-start | bytes 245764 | tf_op jit(solution)/shard_map/while
  217.3 7.0 copy-start.1
  224.3 6.2 copy-start.16
  244.7 7.0 copy-start.1
  251.7 6.2 copy-start.16
  267.7 9.8 copy-start.43
  272.5 5.0 copy-start.11
  277.5 15.4 %copy-start.12 = (bf16[2,1024,10,32]{1,3,2,0:T(8,128)(2,1)}, bf16[2,1024,10,32]{1,3,2,0:T(8,128)(2,1)S(1)}, u32[]{:S(2)}) copy-start(bf16[2,1024,10,32]{1,3,2,0:T(8,128)(2,1)S(1)} %get-tuple-element.1151) | copy-start | bytes 3932164
  282.9 10.0 copy-start.39
  292.9 4.8 copy-start.29
  292.9 5.5 copy-start.24
  292.9 6.3 copy-start.22
  297.6 235.5 %all-reduce.13.cloned.1.call-start = ((), (), s32[]{:S(2)}) async-start(), calls=%async_computation.2 | async-start | bytes 5242880 | tf_op jit(solution)/shard_map/psum | solution.py:233
  300.1 102.0 %copy-start.4 = (bf16[2048,640]{1,0:T(8,128)(2,1)S(1)}, bf16[2048,640]{1,0:T(8,128)(2,1)}, u32[]{:S(2)}) copy-start(bf16[2048,640]{1,0:T(8,128)(2,1)} %param.26) | copy-start | bytes 7864324
  300.1 102.0 %copy-start.46 = (f32[640]{0:T(1024)S(1)}, f32[640]{0:T(1024)}, u32[]{:S(2)}) copy-start(f32[640]{0:T(1024)} %get-tuple-element.569) | copy-start | bytes 7684
  406.6 31.5 %copy-start.32 = (bf16[2048,640]{1,0:T(8,128)(2,1)S(1)}, bf16[2048,640]{1,0:T(8,128)(2,1)}, u32[]{:S(2)}) copy-start(bf16[2048,640]{1,0:T(8,128)(2,1)} %param.27) | copy-start | bytes 7864324
  458.5 604.1 %all-reduce.15.cloned.1.call-start = ((), (), s32[]{:S(2)}) async-start(), calls=%async_computation.3 | async-start | bytes 20971520 | tf_op jit(solution)/shard_map/psum | solution.py:282
  459.0 7.4 copy-start.8
  459.0 7.4 copy-start.68
  533.0 5.1 copy-start.9
  533.0 5.1 copy-start.14
  569.9 7.0 copy-start
  599.7 14.6 %copy-start.2 = (bf16[2,512,10,32]{1,3,2,0:T(8,128)(2,1)S(1)}, bf16[2,512,10,32]{1,3,2,0:T(8,128)(2,1)}, u32[]{:S(2)}) copy-start(bf16[2,512,10,32]{1,3,2,0:T(8,128)(2,1)} %get-tuple-element.1031) | copy-start | bytes 1966084 | tf_op jit(solution)/shard_map/while/body/eval_jaxpr/while
  625.4 7.0 copy-start
  655.5 14.6 %copy-start.2 = (bf16[2,512,10,32]{1,3,2,0:T(8,128)(2,1)S(1)}, bf16[2,512,10,32]{1,3,2,0:T(8,128)(2,1)}, u32[]{:S(2)}) copy-start(bf16[2,512,10,32]{1,3,2,0:T(8,128)(2,1)} %get-tuple-element.1031) | copy-start | bytes 1966084 | tf_op jit(solution)/shard_map/while/body/eval_jaxpr/while
  708.3 7.0 copy-start
  738.1 14.6 %copy-start.2 = (bf16[2,512,10,32]{1,3,2,0:T(8,128)(2,1)S(1)}, bf16[2,512,10,32]{1,3,2,0:T(8,128)(2,1)}, u32[]{:S(2)}) copy-start(bf16[2,512,10,32]{1,3,2,0:T(8,128)(2,1)} %get-tuple-element.1031) | copy-start | bytes 1966084 | tf_op jit(solution)/shard_map/while/body/eval_jaxpr/while
  763.8 7.0 copy-start
  793.8 14.6 %copy-start.2 = (bf16[2,512,10,32]{1,3,2,0:T(8,128)(2,1)S(1)}, bf16[2,512,10,32]{1,3,2,0:T(8,128)(2,1)}, u32[]{:S(2)}) copy-start(bf16[2,512,10,32]{1,3,2,0:T(8,128)(2,1)} %get-tuple-element.1031) | copy-start | bytes 1966084 | tf_op jit(solution)/shard_map/while/body/eval_jaxpr/while
  830.2 8.3 copy-start.19
  830.2 8.3 copy-start.37
  860.1 335.7 %all-reduce.17.cloned.1.call-start = ((), (), s32[]{:S(2)}) async-start(), calls=%async_computation.4 | async-start | bytes 10485760 | tf_op jit(solution)/shard_map/psum | solution.py:218
  860.2 9.0 copy-start.18
  860.2 9.0 copy-start.41
  874.1 188.5 %copy-start.38 = (f32[4,40,320]{2,1,0:T(8,128)S(1)}, f32[4,40,320]{2,1,0:T(8,128)}, u32[]{:S(2)}) copy-start(f32[4,40,320]{2,1,0:T(8,128)} %param.29) | copy-start | bytes 614404
  874.1 191.7 %copy-start.31 = (f32[2,40,1280]{2,1,0:T(8,128)S(1)}, f32[2,40,1280]{2,1,0:T(8,128)}, u32[]{:S(2)}) copy-start(f32[2,40,1280]{2,1,0:T(8,128)} %param.30) | copy-start | bytes 1228804
  880.6 319.2 %copy-start.53 = (f32[2048]{0:T(1024)S(1)}, f32[2048]{0:T(1024)}, u32[]{:S(2)}) copy-start(f32[2048]{0:T(1024)} %copy-done.52) | copy-start | bytes 24580
  1199.2 131.8 %copy-start.47 = (f32[640]{0:T(1024)S(1)}, f32[640]{0:T(1024)}, u32[]{:S(2)}) copy-start(f32[640]{0:T(1024)} %get-tuple-element.569) | copy-start | bytes 7684
  (33 other events, 90.8 us)
Sparse Core Ops, SparseCore 0:
  10.9 94.5 all-gather.1
  297.7 104.3 all-reduce.10
  458.7 74.3 all-reduce.12
  860.2 202.3 all-reduce.14
  1065.7 130.0 all-reduce.16
